TPU v7x, 128 devices: a whole 4x4x4 slice. The times are simulated.
128 devices in a mesh: dp: 16 (over y, x), expert: 8 (over z, core).
Axes of the slice: x: 4, y: 4, z: 4, core: 2. Of those that a mesh axis runs over, the one named last changes fastest.
Arguments:
- tokens: bfloat16 [4096, 4096], P('dp', 'expert'), may hold values from -100 to 100
- w_gate: bfloat16 [8, 4096, 14336], P('expert', None, 'dp'), may hold values from -0.09375 to 0.09375
- w_up: bfloat16 [8, 4096, 14336], P('expert', None, 'dp'), may hold values from -0.09375 to 0.09375
- w_down: bfloat16 [8, 14336, 4096], P('expert', 'dp'), may hold values from -0.046875 to 0.046875
- pick_block: int32 [8, 8], replicated, may hold values from 0 to 3
- pick_live: int32 [8, 8], replicated, may hold values from 0 to 1, as said below
- combine_weight: float32 [8, 8], replicated, may hold values from 0.25 to 1
Outputs:
- combined: bfloat16 [4096, 4096], P('dp', 'expert')
Inputs may be any that keep to these rules, and one draw needn't show every extreme that they name: `pick_live`: each expert takes at least one block, and some expert takes a block from every pair of dp rows.
All inputs are finite; a program needn't handle non-finite values.
Results may differ from a plain program's by a relative error of at most 0.02.
Values may be sent and summed in bfloat16 or wider, within the bound.
A program may use at most 128 MiB of HBM per device.

v0:
```python
import jax
import jax.numpy as jnp
from jax import lax
from jax.sharding import PartitionSpec as P

BLOCK = 128


def from_partner(value, axis, stride):
    return lax.ppermute(value, axis, [(i, i ^ 1 << stride) for i in range(lax.axis_size(axis))])


def rms_normalize(values, square_sums, model_width):
    values_f32 = values.astype(jnp.float32)
    inv_rms = lax.rsqrt(square_sums / model_width + 1e-05)
    return (values_f32 * inv_rms[:, None]).astype(jnp.bfloat16)


def on_device(tokens, w_gate, w_up, w_down, pick_block, pick_live, combine_weight):
    expert_count = lax.axis_size("expert")
    features_dev = tokens.shape[1]
    model_width = features_dev * expert_count
    blocks_here = tokens.shape[0] // BLOCK
    half_rows = BLOCK // 2
    row_index = lax.axis_index("dp")
    half_bit = row_index % 2
    pair_index = row_index // 2
    tokens_f32 = tokens.astype(jnp.float32)
    square_sums = lax.psum(jnp.sum(tokens_f32 * tokens_f32, axis=1), "expert")
    source = rms_normalize(tokens, square_sums, model_width)
    picked = lax.dynamic_index_in_dim(pick_block, pair_index, axis=1, keepdims=False)
    live_flags = lax.dynamic_index_in_dim(pick_live, pair_index, axis=1, keepdims=False)
    weights_here = lax.dynamic_index_in_dim(combine_weight, pair_index, axis=1, keepdims=False)
    owned_here = (live_flags == 1) & (picked // blocks_here == half_bit)
    local_block = picked % blocks_here
    blocks = source.reshape(blocks_here, BLOCK, features_dev)
    chosen = jnp.take(blocks, local_block, axis=0)
    chosen = jnp.where(owned_here[:, None, None], chosen, jnp.zeros((), jnp.bfloat16))
    arrived = lax.all_to_all(chosen, "expert", split_axis=0, concat_axis=2, tiled=True)[0]
    outgoing = lax.dynamic_slice_in_dim(arrived, (1 - half_bit) * half_rows, half_rows, 0)
    partner = from_partner(outgoing, "dp", 0)
    own_half = lax.dynamic_slice_in_dim(arrived, half_bit * half_rows, half_rows, 0)
    merged = own_half + partner
    gate_weights = w_gate[0]
    up_weights = w_up[0]
    down_weights = w_down[0]
    rows_piece = lax.all_gather(merged, "dp", axis=0, tiled=True)
    gate_proj = jnp.dot(rows_piece, gate_weights, preferred_element_type=jnp.float32)
    up_proj = jnp.dot(rows_piece, up_weights, preferred_element_type=jnp.float32)
    hidden = (jax.nn.silu(gate_proj) * up_proj).astype(jnp.bfloat16)
    partial_value = jnp.dot(hidden, down_weights, preferred_element_type=jnp.float32).astype(
        jnp.bfloat16
    )
    summed = lax.psum_scatter(
        lax.optimization_barrier(partial_value).astype(jnp.float32).astype(jnp.bfloat16),
        "dp",
        scatter_dimension=0,
        tiled=True,
    )
    spread = lax.all_to_all(summed[:, None, :], "expert", split_axis=2, concat_axis=1, tiled=True)
    other_half = from_partner(spread, "dp", 0)
    assembled = jnp.where(
        half_bit == 0,
        jnp.concatenate([spread, other_half], axis=0),
        jnp.concatenate([other_half, spread], axis=0),
    )
    slot_match = local_block[None, :] == jnp.arange(blocks_here, dtype=jnp.int32)[:, None]
    combine_coef = jnp.where(
        slot_match & owned_here[None, :], weights_here[None, :], jnp.zeros((), jnp.float32)
    )
    combined = jnp.einsum("le,red->lrd", combine_coef, assembled.astype(jnp.float32))
    return combined.astype(jnp.bfloat16).reshape(blocks_here * BLOCK, features_dev)


def solution(mesh):
    in_specs = (
        P("dp", "expert"),
        P("expert", None, "dp"),
        P("expert", None, "dp"),
        P("expert", "dp", None),
        P(),
        P(),
        P(),
    )
    out_specs = P("dp", "expert")
    return jax.shard_map(
        on_device, mesh=mesh, in_specs=in_specs, out_specs=out_specs, check_vma=False
    )
```

profile of v0, /device:TPU:0, one launch (start us, length us, event | category | flops | bytes accessed | tf_op | source)
XLA Modules:
  0.0 329.2 jit_solution(12364163355996505817)
XLA Ops:
  6.5 0.9 dynamic-slice_reduce_fusion.1
  7.5 1.1 fusion.12
  8.6 16.0 %psum.7 = f32[256]{0:T(256)S(1)} all-reduce(f32[256]{0:T(256)S(1)} %fusion.12), channel_id=1, replica_groups=mesh['dp'=16,'expert'=8] {'expert'}, use_global_device_ids=true, to_apply=%region_1.2 | all-reduce | flops 256 | bytes 2048 | tf_op jit(solution)/shard_map/psum | solution.py:29
  24.5 1.1 fusion.13
  25.6 0.9 fusion.15
  26.5 0.6 gather_fusion
  27.2 1.2 select_select_fusion
  28.4 3.6 %all-to-all-start = ((bf16[8,128,512]{2,1,0:T(8,128)(2,1)}), bf16[8,128,512]{2,1,0:T(8,128)(2,1)S(1)}, u32[]{:S(2)}, u32[]{:S(2)}) async-start(bf16[8,128,512]{2,1,0:T(8,128)(2,1)} %select_select_fusion), calls=%async_computation | async-start | bytes 2097152 | tf_op jit(solution)/shard_map/all_to_all | solution.py:39
  32.0 15.8 %all-to-all-done = bf16[8,128,512]{2,1,0:T(8,128)(2,1)S(1)} async-done(((bf16[8,128,512]{2,1,0:T(8,128)(2,1)}), bf16[8,128,512]{2,1,0:T(8,128)(2,1)S(1)}, u32[]{:S(2)}, u32[]{:S(2)}) %all-to-all-start) | async-done | bytes 1048608 | tf_op jit(solution)/shard_map/all_to_all | solution.py:39
  47.8 0.7 copy.27
  48.5 0.6 constant_dynamic-slice_fusion
  49.1 0.4 copy.29
  49.5 1.6 collective-permute-start
  51.0 0.4 copy.33
  51.4 11.6 %collective-permute-done = bf16[64,4096]{1,0:T(8,128)(2,1)S(1)} collective-permute-done((bf16[64,4096]{1,0:T(8,128)(2,1)S(1)}, bf16[64,4096]{1,0:T(8,128)(2,1)S(1)}, u32[]{:S(2)}, u32[]{:S(2)}) %collective-permute-start) | collective-permute-done | bytes 524320 | tf_op jit(solution)/shard_map/ppermute | solution.py:10
  63.0 1.0 add.73
  64.2 70.0 %all-gather.2.cloned.1.call-done = bf16[1024,4096]{1,0:T(8,128)(2,1)} async-done(((bf16[64,4096]{1,0:T(8,128)(2,1)}), bf16[1024,4096]{1,0:T(8,128)(2,1)}) %all-gather.2.cloned.1.call-update) | async-done | bytes 8388624 | tf_op jit(solution)/shard_map/all_gather | solution.py:47
  134.3 12.5 %fusion.1 = f32[1024,896]{1,0:T(8,128)S(1)} fusion(bf16[1024,4096]{1,0:T(8,128)(2,1)} %all-gather.2.cloned.1.call-done, bf16[1,4096,896]{2,1,0:T(8,128)(2,1)} %param.9), kind=kOutput, calls=%fused_computation.3 | convolution fusion | flops 7516192768 | bytes 19398656 | tf_op jit(solution)/shard_map/dot_general | solution.py:49
  146.8 15.1 %fusion.3 = f32[1024,896]{1,0:T(8,128)S(1)} fusion(bf16[1024,4096]{1,0:T(8,128)(2,1)S(1)} %copy-done.1, bf16[1,4096,896]{2,1,0:T(8,128)(2,1)} %param.8), kind=kOutput, calls=%fused_computation.5 | convolution fusion | flops 7516192768 | bytes 19398656 | tf_op jit(solution)/shard_map/dot_general | solution.py:48
  161.9 14.1 %convolution_convert_fusion = bf16[1024,4096]{1,0:T(8,128)(2,1)} fusion(bf16[1,896,4096]{2,1,0:T(8,128)(2,1)} %param.10, f32[1024,896]{1,0:T(8,128)S(1)} %fusion.1, f32[1024,896]{1,0:T(8,128)S(1)} %fusion.3), kind=kOutput, calls=%fused_computation.1 | convolution fusion | flops 7525892096 | bytes 23068672 | tf_op jit(solution)/shard_map/dot_general | solution.py:51
  176.0 84.8 %reduce-scatter.2.cloned.1.call-done = bf16[64,4096]{1,0:T(8,128)(2,1)} async-done(((bf16[1024,4096]{1,0:T(8,128)(2,1)}), bf16[64,4096]{1,0:T(8,128)(2,1)}) %reduce-scatter.2.cloned.1.call-update) | async-done | bytes 524304 | tf_op jit(solution)/shard_map/reduce_scatter | solution.py:54
  260.7 4.9 %copy.30 = bf16[64,1,4096]{0,1,2:T(2,128)(2,1)S(1)} copy(bf16[64,1,4096]{2,0,1:T(8,128)(2,1)} %bitcast.33) | data formatting | bytes 1048576 | tf_op jit(solution)/shard_map/broadcast_in_dim | solution.py:60
  265.6 0.5 broadcast.170
  266.1 22.6 %reduce.10 = bf16[4096,64]{1,0:T(8,128)(2,1)S(1)} reduce(bf16[4096,1,64]{2,1,0:T(2,128)(2,1)S(1)} %bitcast.29, bf16[]{:T(256)} %broadcast.170), dimensions={1}, to_apply=%bitcast.23.reduce_sub_computation | reduce | bytes 1048578
  288.8 0.7 reshape.126
  289.5 14.6 %all_to_all.27 = bf16[8,2,16384]{2,1,0:T(2,128)(2,1)S(1)} all-to-all(bf16[8,2,16384]{2,1,0:T(2,128)(2,1)S(1)} %reshape.126), channel_id=1, replica_groups=mesh['dp'=16,'expert'=8] {'expert'}, dimensions={0} | all-to-all | bytes 1048576 | tf_op jit(solution)/shard_map/all_to_all | solution.py:60
  304.1 1.2 reshape.127
  305.4 2.3 copy.31
  307.8 1.5 collective-permute-start.1
  309.5 11.7 %collective-permute-done.1 = bf16[64,8,512]{2,1,0:T(8,128)(2,1)S(1)} collective-permute-done((bf16[64,8,512]{2,1,0:T(8,128)(2,1)S(1)}, bf16[64,8,512]{2,1,0:T(8,128)(2,1)S(1)}, u32[]{:S(2)}, u32[]{:S(2)}) %collective-permute-start.1) | collective-permute-done | bytes 524320 | tf_op jit(solution)/shard_map/ppermute | solution.py:10
  321.2 0.4 convolution_convert_fusion.1
  321.6 0.7 copy.32
  (14 shorter events, 0.7 us)
Async XLA Ops:
  6.5 302.8 %copy-start = (f32[8,8]{1,0:T(8,128)S(1)}, f32[8,8]{1,0:T(8,128)}, u32[]{:S(2)}) copy-start(f32[8,8]{1,0:T(8,128)} %param.13) | copy-start | bytes 772
  28.4 19.4 %all-to-all-start = ((bf16[8,128,512]{2,1,0:T(8,128)(2,1)}), bf16[8,128,512]{2,1,0:T(8,128)(2,1)S(1)}, u32[]{:S(2)}, u32[]{:S(2)}) async-start(bf16[8,128,512]{2,1,0:T(8,128)(2,1)} %select_select_fusion), calls=%async_computation | async-start | bytes 2097152 | tf_op jit(solution)/shard_map/all_to_all | solution.py:39
  31.9 102.4 %all-gather.2.cloned.1.call-start = ((), (), s32[]{:S(2)}) async-start(), calls=%async_computation.3 | async-start | bytes 8912896 | tf_op jit(solution)/shard_map/all_gather | solution.py:47
  49.5 13.5 %collective-permute-start = (bf16[64,4096]{1,0:T(8,128)(2,1)S(1)}, bf16[64,4096]{1,0:T(8,128)(2,1)S(1)}, u32[]{:S(2)}, u32[]{:S(2)}) collective-permute-start(bf16[64,4096]{1,0:T(8,128)(2,1)S(1)} %copy.29), channel_id=1, source_target_pairs={{0,8},{8,0},{16,24},{24,16},{32,40},{40,32},{48,56},{56,48},{64,72... | collective-permute-start | bytes 1572872 | tf_op jit(solution)/shard_map/ppermute | solution.py:10
  64.0 196.7 %reduce-scatter.2.cloned.1.call-start = ((), (), s32[]{:S(2)}) async-start(), calls=%async_computation.4 | async-start | bytes 8912896 | tf_op jit(solution)/shard_map/reduce_scatter | solution.py:54
  134.3 12.5 %copy-start.1 = (bf16[1024,4096]{1,0:T(8,128)(2,1)S(1)}, bf16[1024,4096]{1,0:T(8,128)(2,1)}, u32[]{:S(2)}) copy-start(bf16[1024,4096]{1,0:T(8,128)(2,1)} %all-gather.2.cloned.1.call-done) | copy-start | bytes 25165828
  307.8 13.4 %collective-permute-start.1 = (bf16[64,8,512]{2,1,0:T(8,128)(2,1)S(1)}, bf16[64,8,512]{2,1,0:T(8,128)(2,1)S(1)}, u32[]{:S(2)}, u32[]{:S(2)}) collective-permute-start(bf16[64,8,512]{2,1,0:T(8,128)(2,1)S(1)} %bitcast.34), channel_id=1, source_target_pairs={{0,8},{8,0},{16,24},{24,16},{32,40},{40,32},{48,56},{56,48},{64,72... | collective-permute-start | bytes 1572872 | tf_op jit(solution)/shard_map/ppermute | solution.py:10
Sparse Core Ops, SparseCore 0:
  64.1 70.0 all-gather.1
  176.1 84.5 reduce-scatter.1
where the time goes:
time: 330 us; the launch traced here: 329 us
  waiting for transfers between devices  194 us (59%)
  matrix products  42.1 us (13%)
  blocking collectives  30.6 us (9%)
  other arithmetic  28.8 us (9%)
  between operations  13.6 us (4%)
  local copies, waits for them, and re-layouts  13.3 us (4%)
  starting transfers between devices  6.86 us (2%)
    reduce_scatter x1, waiting for transfers between devices, on_device(): lax.psum_scatter(lax.optimization_barrier(partial_value).astype(jnp.float...  84.8 us
    all_gather x1, waiting for transfers between devices, on_device(): rows_piece = lax.all_gather(merged, 'dp', axis=0, tiled=True)  70 us
    ppermute x2, waiting for transfers between devices, from_partner(): lax.ppermute(value, axis, [(i, i ^ 1 << stride) for i in range(lax.axis_s...  23.3 us
    unnamed x1, other arithmetic  22.6 us
    psum x1, blocking collectives, on_device(): square_sums = lax.psum(jnp.sum(tokens_f32 * tokens_f32, axis=1), 'expert')  16 us
    all_to_all x1, waiting for transfers between devices, on_device(): lax.all_to_all(chosen, 'expert', split_axis=0, concat_axis=2, tiled=True)[0]  15.8 us
    dot_general x1, matrix products, on_device(): jnp.dot(rows_piece, gate_weights, preferred_element_type=jnp.float32)  15.1 us
    all_to_all x1, blocking collectives, on_device(): lax.all_to_all(summed[:, None, :], 'expert', split_axis=2, concat_axis=1,...  14.6 us
  transfers between devices with their start and end apart: 5, of which 5 were waited for; matrix products, arithmetic and copies ran while one was open for 0% of the time, Pallas kernels for 0%

commit v1 on v0

--- a/solution.py
+++ b/solution.py
@@ -4,6 +4,19 @@
 from jax.sharding import PartitionSpec as P
 
 BLOCK = 128
+
+
+def ring_gather(array, axis, dim):
+    ways = lax.axis_size(axis)
+    up = [(d, (d + 1) % ways) for d in range(ways)]
+    down = [(d, (d - 1) % ways) for d in range(ways)]
+    earlier, later = ([array], [array])
+    for _ in range(ways // 2):
+        earlier.append(lax.ppermute(earlier[-1], axis, up))
+    for _ in range((ways - 1) // 2):
+        later.append(lax.ppermute(later[-1], axis, down))
+    line = jnp.concatenate([*earlier[::-1], *later[1:]], axis=dim)
+    return jnp.roll(line, (lax.axis_index(axis) - ways // 2) * array.shape[dim], axis=dim)
 
 
 def from_partner(value, axis, stride):
@@ -44,7 +57,7 @@
     gate_weights = w_gate[0]
     up_weights = w_up[0]
     down_weights = w_down[0]
-    rows_piece = lax.all_gather(merged, "dp", axis=0, tiled=True)
+    rows_piece = ring_gather(merged, "dp", 0)
     gate_proj = jnp.dot(rows_piece, gate_weights, preferred_element_type=jnp.float32)
     up_proj = jnp.dot(rows_piece, up_weights, preferred_element_type=jnp.float32)
     hidden = (jax.nn.silu(gate_proj) * up_proj).astype(jnp.bfloat16)

time: 330 us -> 377 us (1.14)
  starting transfers between devices: 6.86 us -> 47.1 us
  local copies, waits for them, and re-layouts: 13.3 us -> 29.9 us
  waiting for transfers between devices: 194 us -> 188 us
  matrix products: 42.1 us -> 37.9 us
    all_gather x1 -> x0, waiting for transfers between devices: 70 us -> none  [on_device(): rows_piece = lax.all_gather(merged, 'dp', axis=0, tiled=True)]
    ppermute x0 -> x15, waiting for transfers between devices: none -> 69.9 us  [the longest x8 66.6 us: ring_gather(): earlier.append(lax.ppermute(earlier[-1], axis, up))]
    ppermute x0 -> x15, starting transfers between devices: none -> 40.4 us  [the longest x7 38.9 us: ring_gather(): later.append(lax.ppermute(later[-1], axis, down))]
    unnamed x9 -> x66, local copies, waits for them, and re-layouts: 3.01 us -> 19.5 us
    reduce_scatter x1, waiting for transfers between devices: 84.8 us -> 79.3 us  [on_device(): lax.psum_scatter(lax.optimization_barrier(partial_value).astype(jnp.float...]
    dot_general x1, matrix products: 15.1 us -> 10.6 us  [on_device(): jnp.dot(rows_piece, gate_weights, preferred_element_type=jnp.float32)]
    unnamed x1 -> x3, other arithmetic: 22.6 us -> 22.4 us
  transfers between devices with their start and end apart: 5 -> 19, of which waited for: 5 -> 15; matrix products, arithmetic and copies ran while one was open for 0% -> 3% of each run, Pallas kernels for 0% -> 0%
where the time goes in v1:
time: 377 us; the launch traced here: 375 us
  waiting for transfers between devices  188 us (50%)
  starting transfers between devices  47.1 us (12%)
  matrix products  37.9 us (10%)
  blocking collectives  30.6 us (8%)
  local copies, waits for them, and re-layouts  29.9 us (8%)
  other arithmetic  27.7 us (7%)
  between operations  13.9 us (4%)
    reduce_scatter x1, waiting for transfers between devices, on_device(): lax.psum_scatter(lax.optimization_barrier(partial_value).astype(jnp.float...  79.3 us
    ppermute x8, waiting for transfers between devices, ring_gather(): earlier.append(lax.ppermute(earlier[-1], axis, up))  66.6 us
    ppermute x7, starting transfers between devices, ring_gather(): later.append(lax.ppermute(later[-1], axis, down))  38.9 us
    ppermute x2, waiting for transfers between devices, from_partner(): lax.ppermute(value, axis, [(i, i ^ 1 << stride) for i in range(lax.axis_s...  23.3 us
    unnamed x3, other arithmetic  22.4 us
    unnamed x66, local copies, waits for them, and re-layouts  19.5 us
    psum x1, blocking collectives, on_device(): square_sums = lax.psum(jnp.sum(tokens_f32 * tokens_f32, axis=1), 'expert')  16 us
    all_to_all x1, waiting for transfers between devices, on_device(): lax.all_to_all(chosen, 'expert', split_axis=0, concat_axis=2, tiled=True)[0]  15.8 us
  transfers between devices with their start and end apart: 19, of which 15 were waited for; matrix products, arithmetic and copies ran while one was open for 3% of the time, Pallas kernels for 0%

profile of v1, /device:TPU:0, one launch (start us, length us, event | category | flops | bytes accessed | tf_op | source)
XLA Modules:
  0.0 375.5 jit_solution(10223533661852071113)
XLA Ops:
  8.6 16.0 %psum.7 = f32[256]{0:T(256)S(1)} all-reduce(f32[256]{0:T(256)S(1)} %fusion.14), channel_id=1, replica_groups=mesh['dp'=16,'expert'=8] {'expert'}, use_global_device_ids=true, to_apply=%region_1.2 | all-reduce | flops 256 | bytes 2048 | tf_op jit(solution)/shard_map/psum | solution.py:42
  28.4 3.6 all-to-all-start
  32.0 15.8 %all-to-all-done = bf16[8,128,512]{2,1,0:T(8,128)(2,1)S(1)} async-done(((bf16[8,128,512]{2,1,0:T(8,128)(2,1)}), bf16[8,128,512]{2,1,0:T(8,128)(2,1)S(1)}, u32[]{:S(2)}, u32[]{:S(2)}) %all-to-all-start) | async-done | bytes 1048608 | tf_op jit(solution)/shard_map/all_to_all | solution.py:52
  49.5 1.6 collective-permute-start
  51.4 11.6 %collective-permute-done = bf16[64,4096]{1,0:T(8,128)(2,1)S(1)} collective-permute-done((bf16[64,4096]{1,0:T(8,128)(2,1)S(1)}, bf16[64,4096]{1,0:T(8,128)(2,1)S(1)}, u32[]{:S(2)}, u32[]{:S(2)}) %collective-permute-start) | collective-permute-done | bytes 524320 | tf_op jit(solution)/shard_map/ppermute | solution.py:23
  63.2 1.6 collective-permute-start.1
  64.7 14.5 %collective-permute-done.1 = bf16[64,4096]{1,0:T(8,128)(2,1)S(1)} collective-permute-done((bf16[64,4096]{1,0:T(8,128)(2,1)S(1)}, bf16[64,4096]{1,0:T(8,128)(2,1)S(1)}, u32[]{:S(2)}, u32[]{:S(2)}) %collective-permute-start.1) | collective-permute-done | bytes 524320 | tf_op jit(solution)/shard_map/ppermute | solution.py:15
  79.3 5.3 %collective-permute-start.9 = (bf16[64,4096]{1,0:T(8,128)(2,1)S(1)}, bf16[64,4096]{1,0:T(8,128)(2,1)S(1)}, u32[]{:S(2)}, u32[]{:S(2)}) collective-permute-start(bf16[64,4096]{1,0:T(8,128)(2,1)S(1)} %add.84), channel_id=1, source_target_pairs={{0,120},{8,0},{16,8},{24,16},{32,24},{40,32},{48,40},{56,48},{64,5... | collective-permute-start | bytes 1572872 | tf_op jit(solution)/shard_map/ppermute | solution.py:17
  84.6 9.8 %collective-permute-done.2 = bf16[64,4096]{1,0:T(8,128)(2,1)S(1)} collective-permute-done((bf16[64,4096]{1,0:T(8,128)(2,1)S(1)}, bf16[64,4096]{1,0:T(8,128)(2,1)S(1)}, u32[]{:S(2)}, u32[]{:S(2)}) %collective-permute-start.2) | collective-permute-done | bytes 524320 | tf_op jit(solution)/shard_map/ppermute | solution.py:15
  94.4 5.3 %collective-permute-start.10 = (bf16[64,4096]{1,0:T(8,128)(2,1)S(1)}, bf16[64,4096]{1,0:T(8,128)(2,1)S(1)}, u32[]{:S(2)}, u32[]{:S(2)}) collective-permute-start(bf16[64,4096]{1,0:T(8,128)(2,1)S(1)} %collective-permute-done.9), channel_id=1, source_target_pairs={{0,120},{8,0},{16,8},{24,16},{32,24},{40,32},{48,40},{56,48},{64,5... | collective-permute-start | bytes 1572872 | tf_op jit(solution)/shard_map/ppermute | solution.py:17
  99.7 8.8 %collective-permute-done.3 = bf16[64,4096]{1,0:T(8,128)(2,1)S(1)} collective-permute-done((bf16[64,4096]{1,0:T(8,128)(2,1)S(1)}, bf16[64,4096]{1,0:T(8,128)(2,1)S(1)}, u32[]{:S(2)}, u32[]{:S(2)}) %collective-permute-start.3) | collective-permute-done | bytes 524320 | tf_op jit(solution)/shard_map/ppermute | solution.py:15
  108.6 5.3 %collective-permute-start.11 = (bf16[64,4096]{1,0:T(8,128)(2,1)S(1)}, bf16[64,4096]{1,0:T(8,128)(2,1)S(1)}, u32[]{:S(2)}, u32[]{:S(2)}) collective-permute-start(bf16[64,4096]{1,0:T(8,128)(2,1)S(1)} %collective-permute-done.10), channel_id=1, source_target_pairs={{0,120},{8,0},{16,8},{24,16},{32,24},{40,32},{48,40},{56,48},{64,5... | collective-permute-start | bytes 1572872 | tf_op jit(solution)/shard_map/ppermute | solution.py:17
  113.9 7.9 %collective-permute-done.4 = bf16[64,4096]{1,0:T(8,128)(2,1)S(1)} collective-permute-done((bf16[64,4096]{1,0:T(8,128)(2,1)S(1)}, bf16[64,4096]{1,0:T(8,128)(2,1)S(1)}, u32[]{:S(2)}, u32[]{:S(2)}) %collective-permute-start.4) | collective-permute-done | bytes 524320 | tf_op jit(solution)/shard_map/ppermute | solution.py:15
  122.7 5.3 %collective-permute-start.12 = (bf16[64,4096]{1,0:T(8,128)(2,1)S(1)}, bf16[64,4096]{1,0:T(8,128)(2,1)S(1)}, u32[]{:S(2)}, u32[]{:S(2)}) collective-permute-start(bf16[64,4096]{1,0:T(8,128)(2,1)S(1)} %collective-permute-done.11), channel_id=1, source_target_pairs={{0,120},{8,0},{16,8},{24,16},{32,24},{40,32},{48,40},{56,48},{64,5... | collective-permute-start | bytes 1572872 | tf_op jit(solution)/shard_map/ppermute | solution.py:17
  128.0 6.3 %collective-permute-done.5 = bf16[64,4096]{1,0:T(8,128)(2,1)S(1)} collective-permute-done((bf16[64,4096]{1,0:T(8,128)(2,1)S(1)}, bf16[64,4096]{1,0:T(8,128)(2,1)S(1)}, u32[]{:S(2)}, u32[]{:S(2)}) %collective-permute-start.5) | collective-permute-done | bytes 524320 | tf_op jit(solution)/shard_map/ppermute | solution.py:15
  135.5 5.8 %collective-permute-start.13 = (bf16[64,4096]{1,0:T(8,128)(2,1)S(1)}, bf16[64,4096]{1,0:T(8,128)(2,1)}, u32[]{:S(2)}, u32[]{:S(2)}) collective-permute-start(bf16[64,4096]{1,0:T(8,128)(2,1)S(1)} %collective-permute-done.12), channel_id=1, source_target_pairs={{0,120},{8,0},{16,8},{24,16},{32,24},{40,32},{48,40},{56,48},{64,5... | collective-permute-start | bytes 1572872 | tf_op jit(solution)/shard_map/ppermute | solution.py:17
  141.3 6.6 %collective-permute-done.6 = bf16[64,4096]{1,0:T(8,128)(2,1)S(1)} collective-permute-done((bf16[64,4096]{1,0:T(8,128)(2,1)S(1)}, bf16[64,4096]{1,0:T(8,128)(2,1)S(1)}, u32[]{:S(2)}, u32[]{:S(2)}) %collective-permute-start.6) | collective-permute-done | bytes 524320 | tf_op jit(solution)/shard_map/ppermute | solution.py:15
  149.1 5.9 %collective-permute-start.14 = (bf16[64,4096]{1,0:T(8,128)(2,1)}, bf16[64,4096]{1,0:T(8,128)(2,1)}, u32[]{:S(2)}, u32[]{:S(2)}) collective-permute-start(bf16[64,4096]{1,0:T(8,128)(2,1)} %collective-permute-done.13), channel_id=1, source_target_pairs={{0,120},{8,0},{16,8},{24,16},{32,24},{40,32},{48,40},{56,48},{64,5... | collective-permute-start | bytes 1572872 | tf_op jit(solution)/shard_map/ppermute | solution.py:17
  155.0 7.4 %collective-permute-done.7 = bf16[64,4096]{1,0:T(8,128)(2,1)} collective-permute-done((bf16[64,4096]{1,0:T(8,128)(2,1)S(1)}, bf16[64,4096]{1,0:T(8,128)(2,1)}, u32[]{:S(2)}, u32[]{:S(2)}) %collective-permute-start.7) | collective-permute-done | bytes 524320 | tf_op jit(solution)/shard_map/ppermute | solution.py:15
  162.4 1.8 collective-permute-done.14
  164.2 5.8 %collective-permute-start.15 = (bf16[64,4096]{1,0:T(8,128)(2,1)}, bf16[64,4096]{1,0:T(8,128)(2,1)S(1)}, u32[]{:S(2)}, u32[]{:S(2)}) collective-permute-start(bf16[64,4096]{1,0:T(8,128)(2,1)} %collective-permute-done.14), channel_id=1, source_target_pairs={{0,120},{8,0},{16,8},{24,16},{32,24},{40,32},{48,40},{56,48},{64,5... | collective-permute-start | bytes 1572872 | tf_op jit(solution)/shard_map/ppermute | solution.py:17
  170.0 5.2 %collective-permute-done.8 = bf16[64,4096]{1,0:T(8,128)(2,1)} collective-permute-done((bf16[64,4096]{1,0:T(8,128)(2,1)}, bf16[64,4096]{1,0:T(8,128)(2,1)}, u32[]{:S(2)}, u32[]{:S(2)}) %collective-permute-start.8) | collective-permute-done | bytes 524320 | tf_op jit(solution)/shard_map/ppermute | solution.py:15
  190.4 10.6 %fusion.2 = f32[1024,896]{1,0:T(8,128)} fusion(bf16[2048,4096]{1,0:T(8,128)(2,1)S(1)} %constant_dynamic-update-slice_fusion, s32[]{:T(128)S(6)} %select_n.103, bf16[1,4096,896]{2,1,0:T(8,128)(2,1)S(1)} %bitcast.35), kind=kOutput, calls=%fused_computation.4 | convolution fusion | flops 7516192768 | bytes 19398660 | tf_op jit(solution)/shard_map/dot_general | solution.py:61
  201.0 12.5 %fusion = f32[1024,896]{1,0:T(8,128)} fusion(bf16[2048,4096]{1,0:T(8,128)(2,1)S(1)} %constant_dynamic-update-slice_fusion, s32[]{:T(128)S(6)} %select_n.103, bf16[1,4096,896]{2,1,0:T(8,128)(2,1)} %param.9), kind=kOutput, calls=%fused_computation.2 | convolution fusion | flops 7516192768 | bytes 19398660 | tf_op jit(solution)/shard_map/dot_general | solution.py:62
  213.5 14.3 %convolution_convert_fusion = bf16[1024,4096]{1,0:T(8,128)(2,1)} fusion(bf16[1,896,4096]{2,1,0:T(8,128)(2,1)S(1)} %bitcast.37, f32[1024,896]{1,0:T(8,128)} %fusion, f32[1024,896]{1,0:T(8,128)} %fusion.2), kind=kOutput, calls=%fused_computation.1 | convolution fusion | flops 7525892096 | bytes 23068672 | tf_op jit(solution)/shard_map/dot_general | solution.py:64
  227.9 79.3 %reduce-scatter.2.cloned.1.call-done = bf16[64,4096]{1,0:T(8,128)(2,1)} async-done(((bf16[1024,4096]{1,0:T(8,128)(2,1)}), bf16[64,4096]{1,0:T(8,128)(2,1)}) %reduce-scatter.2.cloned.1.call-update) | async-done | bytes 524304 | tf_op jit(solution)/shard_map/reduce_scatter | solution.py:67
  307.2 4.9 %copy.92 = bf16[64,1,4096]{0,1,2:T(2,128)(2,1)S(1)} copy(bf16[64,1,4096]{2,0,1:T(8,128)(2,1)} %bitcast.31) | data formatting | bytes 1048576 | tf_op jit(solution)/shard_map/broadcast_in_dim | solution.py:73
  312.6 22.4 %reduce.10 = bf16[4096,64]{1,0:T(8,128)(2,1)S(1)} reduce(bf16[4096,1,64]{2,1,0:T(2,128)(2,1)S(1)} %bitcast.27, bf16[]{:T(256)} %broadcast.171), dimensions={1}, to_apply=%bitcast.23.reduce_sub_computation | reduce | bytes 1048578
  335.7 14.7 %all_to_all.27 = bf16[8,2,16384]{2,1,0:T(2,128)(2,1)S(1)} all-to-all(bf16[8,2,16384]{2,1,0:T(2,128)(2,1)S(1)} %reshape.126), channel_id=1, replica_groups=mesh['dp'=16,'expert'=8] {'expert'}, dimensions={0} | all-to-all | bytes 1048576 | tf_op jit(solution)/shard_map/all_to_all | solution.py:73
  351.6 2.3 copy.93
  354.1 1.5 collective-permute-start.16
  355.7 11.7 %collective-permute-done.16 = bf16[64,8,512]{2,1,0:T(8,128)(2,1)S(1)} collective-permute-done((bf16[64,8,512]{2,1,0:T(8,128)(2,1)S(1)}, bf16[64,8,512]{2,1,0:T(8,128)(2,1)S(1)}, u32[]{:S(2)}, u32[]{:S(2)}) %collective-permute-start.16) | collective-permute-done | bytes 524320 | tf_op jit(solution)/shard_map/ppermute | solution.py:23
  (101 shorter events, 30.1 us)
Async XLA Ops:
  6.5 349.0 %copy-start = (f32[8,8]{1,0:T(8,128)S(1)}, f32[8,8]{1,0:T(8,128)}, u32[]{:S(2)}) copy-start(f32[8,8]{1,0:T(8,128)} %param.13) | copy-start | bytes 772
  28.4 19.4 %all-to-all-start = ((bf16[8,128,512]{2,1,0:T(8,128)(2,1)}), bf16[8,128,512]{2,1,0:T(8,128)(2,1)S(1)}, u32[]{:S(2)}, u32[]{:S(2)}) async-start(bf16[8,128,512]{2,1,0:T(8,128)(2,1)} %select_select_fusion), calls=%async_computation | async-start | bytes 2097152 | tf_op jit(solution)/shard_map/all_to_all | solution.py:52
  31.9 275.3 %reduce-scatter.2.cloned.1.call-start = ((), (), s32[]{:S(2)}) async-start(), calls=%async_computation.3 | async-start | bytes 8912896 | tf_op jit(solution)/shard_map/reduce_scatter | solution.py:67
  49.5 13.5 %collective-permute-start = (bf16[64,4096]{1,0:T(8,128)(2,1)S(1)}, bf16[64,4096]{1,0:T(8,128)(2,1)S(1)}, u32[]{:S(2)}, u32[]{:S(2)}) collective-permute-start(bf16[64,4096]{1,0:T(8,128)(2,1)S(1)} %copy.91), channel_id=1, source_target_pairs={{0,8},{8,0},{16,24},{24,16},{32,40},{40,32},{48,56},{56,48},{64,72... | collective-permute-start | bytes 1572872 | tf_op jit(solution)/shard_map/ppermute | solution.py:23
  63.2 16.1 %collective-permute-start.1 = (bf16[64,4096]{1,0:T(8,128)(2,1)S(1)}, bf16[64,4096]{1,0:T(8,128)(2,1)S(1)}, u32[]{:S(2)}, u32[]{:S(2)}) collective-permute-start(bf16[64,4096]{1,0:T(8,128)(2,1)S(1)} %add.84), channel_id=1, source_target_pairs={{0,8},{8,16},{16,24},{24,32},{32,40},{40,48},{48,56},{56,64},{64,7... | collective-permute-start | bytes 1572872 | tf_op jit(solution)/shard_map/ppermute | solution.py:15
  79.3 15.1 %collective-permute-start.2 = (bf16[64,4096]{1,0:T(8,128)(2,1)S(1)}, bf16[64,4096]{1,0:T(8,128)(2,1)S(1)}, u32[]{:S(2)}, u32[]{:S(2)}) collective-permute-start(bf16[64,4096]{1,0:T(8,128)(2,1)S(1)} %collective-permute-done.1), channel_id=1, source_target_pairs={{0,8},{8,16},{16,24},{24,32},{32,40},{40,48},{48,56},{56,64},{64,7... | collective-permute-start | bytes 1572872 | tf_op jit(solution)/shard_map/ppermute | solution.py:15
  79.3 15.1 %collective-permute-start.9 = (bf16[64,4096]{1,0:T(8,128)(2,1)S(1)}, bf16[64,4096]{1,0:T(8,128)(2,1)S(1)}, u32[]{:S(2)}, u32[]{:S(2)}) collective-permute-start(bf16[64,4096]{1,0:T(8,128)(2,1)S(1)} %add.84), channel_id=1, source_target_pairs={{0,120},{8,0},{16,8},{24,16},{32,24},{40,32},{48,40},{56,48},{64,5... | collective-permute-start | bytes 1572872 | tf_op jit(solution)/shard_map/ppermute | solution.py:17
  94.4 14.2 %collective-permute-start.3 = (bf16[64,4096]{1,0:T(8,128)(2,1)S(1)}, bf16[64,4096]{1,0:T(8,128)(2,1)S(1)}, u32[]{:S(2)}, u32[]{:S(2)}) collective-permute-start(bf16[64,4096]{1,0:T(8,128)(2,1)S(1)} %collective-permute-done.2), channel_id=1, source_target_pairs={{0,8},{8,16},{16,24},{24,32},{32,40},{40,48},{48,56},{56,64},{64,7... | collective-permute-start | bytes 1572872 | tf_op jit(solution)/shard_map/ppermute | solution.py:15
  94.4 14.2 %collective-permute-start.10 = (bf16[64,4096]{1,0:T(8,128)(2,1)S(1)}, bf16[64,4096]{1,0:T(8,128)(2,1)S(1)}, u32[]{:S(2)}, u32[]{:S(2)}) collective-permute-start(bf16[64,4096]{1,0:T(8,128)(2,1)S(1)} %collective-permute-done.9), channel_id=1, source_target_pairs={{0,120},{8,0},{16,8},{24,16},{32,24},{40,32},{48,40},{56,48},{64,5... | collective-permute-start | bytes 1572872 | tf_op jit(solution)/shard_map/ppermute | solution.py:17
  108.6 13.3 %collective-permute-start.4 = (bf16[64,4096]{1,0:T(8,128)(2,1)S(1)}, bf16[64,4096]{1,0:T(8,128)(2,1)S(1)}, u32[]{:S(2)}, u32[]{:S(2)}) collective-permute-start(bf16[64,4096]{1,0:T(8,128)(2,1)S(1)} %collective-permute-done.3), channel_id=1, source_target_pairs={{0,8},{8,16},{16,24},{24,32},{32,40},{40,48},{48,56},{56,64},{64,7... | collective-permute-start | bytes 1572872 | tf_op jit(solution)/shard_map/ppermute | solution.py:15
  108.6 13.3 %collective-permute-start.11 = (bf16[64,4096]{1,0:T(8,128)(2,1)S(1)}, bf16[64,4096]{1,0:T(8,128)(2,1)S(1)}, u32[]{:S(2)}, u32[]{:S(2)}) collective-permute-start(bf16[64,4096]{1,0:T(8,128)(2,1)S(1)} %collective-permute-done.10), channel_id=1, source_target_pairs={{0,120},{8,0},{16,8},{24,16},{32,24},{40,32},{48,40},{56,48},{64,5... | collective-permute-start | bytes 1572872 | tf_op jit(solution)/shard_map/ppermute | solution.py:17
  121.8 27.3 %copy-start.5 = (bf16[64,4096]{1,0:T(8,128)(2,1)}, bf16[64,4096]{1,0:T(8,128)(2,1)S(1)}, u32[]{:S(2)}) copy-start(bf16[64,4096]{1,0:T(8,128)(2,1)S(1)} %collective-permute-done.4) | copy-start | bytes 1572868
  121.8 12.5 %collective-permute-start.5 = (bf16[64,4096]{1,0:T(8,128)(2,1)S(1)}, bf16[64,4096]{1,0:T(8,128)(2,1)S(1)}, u32[]{:S(2)}, u32[]{:S(2)}) collective-permute-start(bf16[64,4096]{1,0:T(8,128)(2,1)S(1)} %collective-permute-done.4), channel_id=1, source_target_pairs={{0,8},{8,16},{16,24},{24,32},{32,40},{40,48},{48,56},{56,64},{64,7... | collective-permute-start | bytes 1572872 | tf_op jit(solution)/shard_map/ppermute | solution.py:15
  122.7 12.0 %collective-permute-start.12 = (bf16[64,4096]{1,0:T(8,128)(2,1)S(1)}, bf16[64,4096]{1,0:T(8,128)(2,1)S(1)}, u32[]{:S(2)}, u32[]{:S(2)}) collective-permute-start(bf16[64,4096]{1,0:T(8,128)(2,1)S(1)} %collective-permute-done.11), channel_id=1, source_target_pairs={{0,120},{8,0},{16,8},{24,16},{32,24},{40,32},{48,40},{56,48},{64,5... | collective-permute-start | bytes 1572872 | tf_op jit(solution)/shard_map/ppermute | solution.py:17
  134.3 20.7 %copy-start.7 = (bf16[64,4096]{1,0:T(8,128)(2,1)}, bf16[64,4096]{1,0:T(8,128)(2,1)S(1)}, u32[]{:S(2)}) copy-start(bf16[64,4096]{1,0:T(8,128)(2,1)S(1)} %collective-permute-done.5) | copy-start | bytes 1572868
  134.3 13.6 %collective-permute-start.6 = (bf16[64,4096]{1,0:T(8,128)(2,1)S(1)}, bf16[64,4096]{1,0:T(8,128)(2,1)S(1)}, u32[]{:S(2)}, u32[]{:S(2)}) collective-permute-start(bf16[64,4096]{1,0:T(8,128)(2,1)S(1)} %collective-permute-done.5), channel_id=1, source_target_pairs={{0,8},{8,16},{16,24},{24,32},{32,40},{40,48},{48,56},{56,64},{64,7... | collective-permute-start | bytes 1572872 | tf_op jit(solution)/shard_map/ppermute | solution.py:15
  135.5 13.6 %collective-permute-start.13 = (bf16[64,4096]{1,0:T(8,128)(2,1)S(1)}, bf16[64,4096]{1,0:T(8,128)(2,1)}, u32[]{:S(2)}, u32[]{:S(2)}) collective-permute-start(bf16[64,4096]{1,0:T(8,128)(2,1)S(1)} %collective-permute-done.12), channel_id=1, source_target_pairs={{0,120},{8,0},{16,8},{24,16},{32,24},{40,32},{48,40},{56,48},{64,5... | collective-permute-start | bytes 1572872 | tf_op jit(solution)/shard_map/ppermute | solution.py:17
  147.9 14.5 %copy-start.9 = (bf16[64,4096]{1,0:T(8,128)(2,1)}, bf16[64,4096]{1,0:T(8,128)(2,1)S(1)}, u32[]{:S(2)}) copy-start(bf16[64,4096]{1,0:T(8,128)(2,1)S(1)} %collective-permute-done.6) | copy-start | bytes 1572868
  147.9 14.4 %collective-permute-start.7 = (bf16[64,4096]{1,0:T(8,128)(2,1)S(1)}, bf16[64,4096]{1,0:T(8,128)(2,1)}, u32[]{:S(2)}, u32[]{:S(2)}) collective-permute-start(bf16[64,4096]{1,0:T(8,128)(2,1)S(1)} %collective-permute-done.6), channel_id=1, source_target_pairs={{0,8},{8,16},{16,24},{24,32},{32,40},{40,48},{48,56},{56,64},{64,7... | collective-permute-start | bytes 1572872 | tf_op jit(solution)/shard_map/ppermute | solution.py:15
  149.1 15.1 %collective-permute-start.14 = (bf16[64,4096]{1,0:T(8,128)(2,1)}, bf16[64,4096]{1,0:T(8,128)(2,1)}, u32[]{:S(2)}, u32[]{:S(2)}) collective-permute-start(bf16[64,4096]{1,0:T(8,128)(2,1)} %collective-permute-done.13), channel_id=1, source_target_pairs={{0,120},{8,0},{16,8},{24,16},{32,24},{40,32},{48,40},{56,48},{64,5... | collective-permute-start | bytes 1572872 | tf_op jit(solution)/shard_map/ppermute | solution.py:17
  162.4 12.8 %collective-permute-start.8 = (bf16[64,4096]{1,0:T(8,128)(2,1)}, bf16[64,4096]{1,0:T(8,128)(2,1)}, u32[]{:S(2)}, u32[]{:S(2)}) collective-permute-start(bf16[64,4096]{1,0:T(8,128)(2,1)} %collective-permute-done.7), channel_id=1, source_target_pairs={{0,8},{8,16},{16,24},{24,32},{32,40},{40,48},{48,56},{56,64},{64,7... | collective-permute-start | bytes 1572872 | tf_op jit(solution)/shard_map/ppermute | solution.py:15
  162.4 25.2 %copy-start.10 = (bf16[64,4096]{1,0:T(8,128)(2,1)S(1)}, bf16[64,4096]{1,0:T(8,128)(2,1)}, u32[]{:S(2)}) copy-start(bf16[64,4096]{1,0:T(8,128)(2,1)} %copy-done.9) | copy-start | bytes 1572868
  162.4 25.3 %copy-start.8 = (bf16[64,4096]{1,0:T(8,128)(2,1)S(1)}, bf16[64,4096]{1,0:T(8,128)(2,1)}, u32[]{:S(2)}) copy-start(bf16[64,4096]{1,0:T(8,128)(2,1)} %copy-done.7) | copy-start | bytes 1572868
  162.4 25.3 %copy-start.6 = (bf16[64,4096]{1,0:T(8,128)(2,1)S(1)}, bf16[64,4096]{1,0:T(8,128)(2,1)}, u32[]{:S(2)}) copy-start(bf16[64,4096]{1,0:T(8,128)(2,1)} %copy-done.5) | copy-start | bytes 1572868
  162.4 25.6 %copy-start.2 = (bf16[64,4096]{1,0:T(8,128)(2,1)S(1)}, bf16[64,4096]{1,0:T(8,128)(2,1)}, u32[]{:S(2)}) copy-start(bf16[64,4096]{1,0:T(8,128)(2,1)} %copy-done.1) | copy-start | bytes 1572868
  162.4 25.6 %copy-start.4 = (bf16[64,4096]{1,0:T(8,128)(2,1)S(1)}, bf16[64,4096]{1,0:T(8,128)(2,1)}, u32[]{:S(2)}) copy-start(bf16[64,4096]{1,0:T(8,128)(2,1)} %copy-done.3) | copy-start | bytes 1572868
  162.4 27.9 %slice-start = ((s8[7340032]{0:T(1024)(128)(4,1)}), s8[4194304]{0:T(1024)(128)(4,1)S(1)}, s32[]{:S(2)}) async-start(s8[7340032]{0:T(1024)(128)(4,1)} %bitcast.34), calls=%async_computation.4 | async-start | bytes 8388608
  164.2 21.0 %collective-permute-start.15 = (bf16[64,4096]{1,0:T(8,128)(2,1)}, bf16[64,4096]{1,0:T(8,128)(2,1)S(1)}, u32[]{:S(2)}, u32[]{:S(2)}) collective-permute-start(bf16[64,4096]{1,0:T(8,128)(2,1)} %collective-permute-done.14), channel_id=1, source_target_pairs={{0,120},{8,0},{16,8},{24,16},{32,24},{40,32},{48,40},{56,48},{64,5... | collective-permute-start | bytes 1572872 | tf_op jit(solution)/shard_map/ppermute | solution.py:17
  185.3 5.1 %slice-start.1 = ((s8[7340032]{0:T(1024)(128)(4,1)}), s8[3145728]{0:T(1024)(128)(4,1)S(1)}, s32[]{:S(2)}) async-start(s8[7340032]{0:T(1024)(128)(4,1)} %bitcast.34), calls=%async_computation.5 | async-start | bytes 6291456
  190.4 23.2 %slice-start.2 = ((s8[7340032]{0:T(1024)(128)(4,1)}), s8[3145728]{0:T(1024)(128)(4,1)S(1)}, s32[]{:S(2)}) async-start(s8[7340032]{0:T(1024)(128)(4,1)} %bitcast.36), calls=%async_computation.6 | async-start | bytes 6291456
  201.0 12.5 %slice-start.3 = ((s8[7340032]{0:T(1024)(128)(4,1)}), s8[4194304]{0:T(1024)(128)(4,1)S(1)}, s32[]{:S(2)}) async-start(s8[7340032]{0:T(1024)(128)(4,1)} %bitcast.36), calls=%async_computation.7 | async-start | bytes 8388608
  354.1 13.4 %collective-permute-start.16 = (bf16[64,8,512]{2,1,0:T(8,128)(2,1)S(1)}, bf16[64,8,512]{2,1,0:T(8,128)(2,1)S(1)}, u32[]{:S(2)}, u32[]{:S(2)}) collective-permute-start(bf16[64,8,512]{2,1,0:T(8,128)(2,1)S(1)} %bitcast.32), channel_id=1, source_target_pairs={{0,8},{8,0},{16,24},{24,16},{32,40},{40,32},{48,56},{56,48},{64,72... | collective-permute-start | bytes 1572872 | tf_op jit(solution)/shard_map/ppermute | solution.py:23
  (2 other events, 1.7 us)
Sparse Core Ops, SparseCore 0:
  228.0 79.1 reduce-scatter.1
